TPU v7x, 512 devices: a whole 4x4x16 slice. The times are simulated.
512 devices in a mesh: layer: 16 (over z_hi, y), latent: 32 (over z_lo, x, core).
Axes of the slice: x: 4, y: 4, z: 16 (z_hi: 4, z_lo: 4; z = z_hi * 4 + z_lo), core: 2. Of those that a mesh axis runs over, the one named last changes fastest.
Arguments:
- acts: bfloat16 [512, 16, 2304], P('latent', 'layer'), may hold values from -6 to 6
- enc_weight: bfloat16 [16, 2304, 16384], P('layer', None, 'latent'), may hold values from -0.03125 to 0.03125
- enc_bias: float32 [16384], P('latent'), may hold values from -3 to 3
- dec_weight: bfloat16 [16, 16384, 2304], P('layer', 'latent'), may hold values from -0.0625 to 0.0625
- dec_bias: float32 [16, 2304], P('layer'), may hold values from -4 to 4
Outputs:
- recon: bfloat16 [512, 16, 2304], P('latent', 'layer')
All inputs are finite; a program needn't handle non-finite values.
Results may differ from a plain program's by a relative error of at most 0.023.
Values may be sent and summed in bfloat16 or wider, within the bound.
A program may use at most 64 MiB of HBM per device.

v0:
```python
import jax
import jax.numpy as jnp
from jax import lax
from jax.sharding import Mesh
from jax.sharding import PartitionSpec as P

LATENT = ("latent_0", "latent_1", "latent_2")
LAYER = ("layer_0", "layer_1")


def copy_for_each(x, axis):
    count = lax.axis_size(axis)
    return lax.all_to_all(jnp.broadcast_to(x[None], (count, *x.shape)), axis, 0, 0, tiled=True)


def laid_out(pieces, dim):
    lengths = list(pieces.shape[1:])
    lengths[dim] *= pieces.shape[0]
    return jnp.moveaxis(pieces, 0, dim).reshape(lengths)


def whole_of(x, axes, dim):
    far, near = axes
    initial = copy_for_each(x, far)
    pieces = jnp.swapaxes(copy_for_each(initial, near), 0, 1)
    return laid_out(pieces.reshape(-1, *x.shape), dim)


def split_up(x, dim, count):
    lengths = x.shape
    pieces = x.reshape(*lengths[:dim], count, lengths[dim] // count, *lengths[dim + 1 :])
    return jnp.moveaxis(pieces, dim, 0)


def sent_and_summed(x, axis, dim):
    count = lax.axis_size(axis)
    pieces = lax.all_to_all(split_up(x, dim, count), axis, 0, 0, tiled=True)
    return jnp.sum(pieces.astype(jnp.float32), axis=0)


def sum_by_axis(x, axes, dim):
    far, near = axes
    own = sent_and_summed(split_up(x, dim, lax.axis_size(far)), near, dim + 1)
    return jnp.sum(
        lax.all_to_all(own.astype(jnp.bfloat16), far, 0, 0, tiled=True).astype(jnp.float32), axis=0
    )


def padded_to(lines, count):
    spare = -len(lines) % count
    return jnp.pad(lines, [(0, spare)] + [(0, 0)] * (lines.ndim - 1))


def nested_sum(x, axes):
    lines = x.reshape(-1, x.shape[-1])
    own = sum_by_axis(padded_to(lines, lax.axis_size(axes[0]) * lax.axis_size(axes[1])), axes, 0)
    whole = whole_of(own.astype(jnp.bfloat16), axes, 0)
    return whole[: len(lines)].reshape(x.shape).astype(jnp.float32)


def on_device(acts, enc_weight, enc_bias, dec_weight, dec_bias):
    lay_count = acts.shape[1]
    width = acts.shape[2]
    panel = enc_weight.shape[2]
    flat_enc = enc_weight.reshape(lay_count * width, panel)
    piece = whole_of(acts, (("latent_0", "latent_1"), "latent_2"), 0)
    flat_rows = piece.reshape(piece.shape[0], lay_count * width)
    local_pre = jnp.dot(flat_rows, flat_enc, preferred_element_type=jnp.float32)
    summed = nested_sum(local_pre.astype(jnp.bfloat16), ("layer_0", "layer_1"))
    codes = jnp.maximum(summed + enc_bias[None, :], 0.0).astype(jnp.bfloat16)
    total = sent_and_summed(
        jnp.einsum("tk,lkd->tld", codes, dec_weight, preferred_element_type=jnp.float32).astype(
            jnp.bfloat16
        ),
        LATENT,
        0,
    )
    return (total + dec_bias[None, :, :]).astype(jnp.bfloat16)


def solution(mesh):
    finer = Mesh(
        mesh.devices.reshape(4, 4, 4, 4, 2),
        ("layer_0", "layer_1", "latent_0", "latent_1", "latent_2"),
    )
    placed = (
        P(LATENT, LAYER, None),
        P(LAYER, None, LATENT),
        P(LATENT),
        P(LAYER, LATENT, None),
        P(LAYER, None),
    )
    return jax.shard_map(
        on_device, mesh=finer, in_specs=placed, out_specs=P(LATENT, LAYER, None), check_vma=False
    )
```

profile of v0, /device:TPU:1, one launch (start us, length us, event | category | flops | bytes accessed | tf_op | source)
XLA Modules:
  0.0 181.6 jit_solution(12533552751194692645)
XLA Ops:
  0.0 0.0 copy-start
  0.0 1.1 broadcast_in_dim.13
  1.1 38.1 %all_to_all.35 = bf16[16,16,1,2304]{3,1,2,0:T(8,128)(2,1)S(1)} all-to-all(bf16[16,16,1,2304]{3,1,2,0:T(8,128)(2,1)S(1)} %broadcast_in_dim.13), channel_id=1, replica_groups=mesh['layer_0'=4,'layer_1'=4,'latent_0'=4,'latent_1'=4,'latent_2'=2] {'l..., dimensions={0} | all-to-all | bytes 2359296 | tf_op jit(solution)/shard_map/all_to_all | solution.py:13
  39.2 0.2 broadcast_in_dim.15
  39.4 7.2 %all_to_all.36 = bf16[2,16,16,1,2304]{4,2,1,3,0:T(8,128)(2,1)S(1)} all-to-all(bf16[2,16,16,1,2304]{4,2,1,3,0:T(8,128)(2,1)S(1)} %broadcast_in_dim.15), channel_id=1, replica_groups=mesh['layer_0'=4,'layer_1'=4,'latent_0'=4,'latent_1'=4,'latent_2'=2] {'l..., dimensions={0} | all-to-all | bytes 4718592 | tf_op jit(solution)/shard_map/all_to_all | solution.py:13
  46.6 0.0 copy-start.3
  46.6 0.2 copy.10
  46.8 1.4 copy-done.3
  48.3 1.4 fusion.3
  49.7 0.0 copy-start.2
  49.7 12.6 %all_to_all.37 = bf16[4,4,32,512]{3,2,1,0:T(8,128)(2,1)S(1)} all-to-all(bf16[4,4,32,512]{3,2,1,0:T(8,128)(2,1)S(1)} %bitcast.32), channel_id=1, replica_groups=mesh['layer_0'=4,'layer_1'=4,'latent_0'=4,'latent_1'=4,'latent_2'=2] {'l..., dimensions={0} | all-to-all | bytes 1048576 | tf_op jit(solution)/shard_map/all_to_all | solution.py:37
  62.3 0.1 reduce_sum.35
  62.4 24.0 %all_to_all.38 = bf16[4,32,512]{2,1,0:T(8,128)(2,1)S(1)} all-to-all(bf16[4,32,512]{2,1,0:T(8,128)(2,1)S(1)} %reduce_sum.35), channel_id=1, replica_groups=mesh['layer_0'=4,'layer_1'=4,'latent_0'=4,'latent_1'=4,'latent_2'=2] {'l..., dimensions={0} | all-to-all | bytes 262144 | tf_op jit(solution)/shard_map/all_to_all | solution.py:45
  86.4 15.8 %all_to_all.39 = bf16[4,32,512]{2,1,0:T(8,128)(2,1)S(1)} all-to-all(bf16[4,32,512]{2,1,0:T(8,128)(2,1)S(1)} %broadcast_in_dim.16), channel_id=1, replica_groups=mesh['layer_0'=4,'layer_1'=4,'latent_0'=4,'latent_1'=4,'latent_2'=2] {'l..., dimensions={0} | all-to-all | bytes 262144 | tf_op jit(solution)/shard_map/all_to_all | solution.py:13
  102.2 9.3 %all_to_all.40 = bf16[4,4,32,512]{3,2,1,0:T(8,128)(2,1)S(1)} all-to-all(bf16[4,4,32,512]{3,2,1,0:T(8,128)(2,1)S(1)} %broadcast_in_dim.17), channel_id=1, replica_groups=mesh['layer_0'=4,'layer_1'=4,'latent_0'=4,'latent_1'=4,'latent_2'=2] {'l..., dimensions={0} | all-to-all | bytes 1048576 | tf_op jit(solution)/shard_map/all_to_all | solution.py:13
  111.6 0.0 copy-done.2
  111.6 0.1 maximum_convert_fusion
  111.7 0.0 copy-done
  111.7 2.8 %convolution_convert_fusion = bf16[512,2304]{1,0:T(8,128)(2,1)} fusion(bf16[512,512]{1,0:T(8,128)(2,1)S(1)} %bitcast.34, bf16[1,512,2304]{2,1,0:T(8,128)(2,1)S(1)} %copy-done), kind=kOutput, calls=%fused_computation.1 | convolution fusion | flops 1209139200 | bytes 5242880 | tf_op jit(solution)/shard_map/tk,lkd->tld/dot_general | solution.py:72
  114.5 10.8 %all-to-all-start.6 = ((bf16[32,16,1,2304]{3,1,2,0:T(8,128)(2,1)}), bf16[32,16,1,2304]{3,1,2,0:T(8,128)(2,1)}, u32[]{:S(2)}, u32[]{:S(2)}) async-start(bf16[32,16,1,2304]{3,1,2,0:T(8,128)(2,1)} %bitcast.30), calls=%async_computation.6 | async-start | bytes 4718592 | tf_op jit(solution)/shard_map/all_to_all | solution.py:37
  125.3 0.0 copy-done.1
  125.4 53.6 %all-to-all-done.6 = bf16[32,16,1,2304]{3,1,2,0:T(8,128)(2,1)} async-done(((bf16[32,16,1,2304]{3,1,2,0:T(8,128)(2,1)}), bf16[32,16,1,2304]{3,1,2,0:T(8,128)(2,1)}, u32[]{:S(2)}, u32[]{:S(2)}) %all-to-all-start.6) | async-done | bytes 2359328 | tf_op jit(solution)/shard_map/all_to_all | solution.py:37
  179.0 2.0 %convert_reduce_fusion = f32[16,2304]{1,0:T(8,128)S(1)} fusion(bf16[32,16,1,2304]{3,1,2,0:T(8,128)(2,1)} %all-to-all-done.6), kind=kLoop, calls=%fused_computation | loop fusion | flops 2322432 | bytes 2506752 | tf_op jit(solution)/shard_map/reduce_sum | solution.py:38
  181.0 0.6 fusion.6
  (6 shorter events, 0.1 us)
Async XLA Ops:
  0.0 111.7 %copy-start = (bf16[1,512,2304]{2,1,0:T(8,128)(2,1)S(1)}, bf16[1,512,2304]{2,1,0:T(8,128)(2,1)}, u32[]{:S(2)}) copy-start(bf16[1,512,2304]{2,1,0:T(8,128)(2,1)} %param.8) | copy-start | bytes 7077892
  46.6 1.7 copy-start.3
  49.7 61.9 %copy-start.2 = (f32[512]{0:T(512)S(1)}, f32[512]{0:T(512)}, u32[]{:S(2)}) copy-start(f32[512]{0:T(512)} %param.7) | copy-start | bytes 6148
  114.5 10.8 %copy-start.1 = (f32[1,2304]{1,0:T(1,128)S(1)}, f32[1,2304]{1,0:T(1,128)}, u32[]{:S(2)}) copy-start(f32[1,2304]{1,0:T(1,128)} %param.9) | copy-start | bytes 27652
  114.5 64.5 %all-to-all-start.6 = ((bf16[32,16,1,2304]{3,1,2,0:T(8,128)(2,1)}), bf16[32,16,1,2304]{3,1,2,0:T(8,128)(2,1)}, u32[]{:S(2)}, u32[]{:S(2)}) async-start(bf16[32,16,1,2304]{3,1,2,0:T(8,128)(2,1)} %bitcast.30), calls=%async_computation.6 | async-start | bytes 4718592 | tf_op jit(solution)/shard_map/all_to_all | solution.py:37
where the time goes:
time: 182 us
  blocking collectives  107 us (59%)
  waiting for transfers between devices  53.6 us (29%)
  starting transfers between devices  10.8 us (6%)
  matrix products  4.16 us (2%)
  local copies, waits for them, and re-layouts  3.03 us (2%)
  other arithmetic  2.91 us (2%)
    all_to_all x4, blocking collectives, copy_for_each(): lax.all_to_all(jnp.broadcast_to(x[None], (count, *x.shape)), axis, 0, 0,...  70.5 us
    all_to_all x1, waiting for transfers between devices, sent_and_summed(): pieces = lax.all_to_all(split_up(x, dim, count), axis, 0, 0, tiled=True)  53.6 us
    all_to_all x1, blocking collectives, sum_by_axis(): lax.all_to_all(own.astype(jnp.bfloat16), far, 0, 0, tiled=True)  24 us
    all_to_all x1, blocking collectives, sent_and_summed(): pieces = lax.all_to_all(split_up(x, dim, count), axis, 0, 0, tiled=True)  12.6 us
    all_to_all x1, starting transfers between devices, sent_and_summed(): pieces = lax.all_to_all(split_up(x, dim, count), axis, 0, 0, tiled=True)  10.8 us
  transfers between devices with their start and end apart: 1, of which 1 were waited for; matrix products, arithmetic and copies ran while one was open for 0% of the time, Pallas kernels for 0%

commit v1 on v0

v1 whole, which is shorter than its diff:
```python
import jax
import jax.numpy as jnp
from jax import lax
from jax.experimental import pallas as pl
from jax.experimental.pallas import tpu as pltpu
from jax.sharding import PartitionSpec as P

MESH = pl.DeviceIdType.MESH
BF, F32 = jnp.bfloat16, jnp.float32
K = 4
ORDER = (
    "A0", "A1", "Y0", "A2", "B0", "C0", "A3", "B1", "C1", "Z0", "D0", "B2", "C2", "D1", "B3", "C3", "E0",
    "D2", "E1", "D3", "F0", "E2", "F1", "E3", "G0", "F2", "H0", "G1", "F3", "H1", "G2", "I0", "H2", "G3",
    "I1", "H3", "I2", "I3",
)


def kernel(
    acts, wenc, benc, wdec, bdec, out,
    xg, we, wd, be, bd, pre, ps, yr, s1, zs, zr, cod, pb, sr, qb, xr, rb, fr, acc,
    local, known, az_s, az_r, ax_s, ax_r, ac_s, ac_r, y_s, y_r, z_s, z_r, yg_s, yg_r,
    c_s, c_r, x_s, x_r, f_s, f_r,
):
    layer, latent = lax.axis_index("layer"), lax.axis_index("latent")
    zh, y = lax.div(layer, 4), lax.rem(layer, 4)
    zl, x, c = lax.div(latent, 8), lax.rem(lax.div(latent, 2), 4), lax.rem(latent, 2)

    def up(v, n):
        return lax.rem(v + n, 4)

    def at(zh_=zh, y_=y, zl_=zl, x_=x, c_=c):
        return {"layer": zh_ * 4 + y_, "latent": (zl_ * 4 + x_) * 2 + c_}

    def along_z(n):
        z = lax.rem(zh * 4 + zl + 16 + n, 16)
        return at(zh_=lax.div(z, 4), zl_=lax.rem(z, 4))

    shifts = (1, 3, 2)
    sib = at(c_=1 - c)
    xs = [up(x, n) for n in shifts]
    ys = [up(y, n) for n in shifts]
    lows = [zl, zl + 1 - 2 * lax.rem(zl, 2), up(zl, 2), 3 - zl]
    inner, outer = zh + 1 - 2 * lax.rem(zh, 2), 3 - zh
    to_x, to_y = [at(x_=v) for v in xs], [at(y_=v) for v in ys]
    to_pair = [at(zh_=inner + c * (outer - inner)), at(zh_=outer + c * (inner - outer))]
    to_zl = [None] + [at(zl_=v) for v in lows[1:]]

    loads = [
        pltpu.make_async_copy(src, dst, local.at[i])
        for i, (src, dst) in enumerate(
            ((acts, xg.at[0, c, x]), (wenc, we), (wdec, wd), (benc, be), (bdec, bd))
        )
    ]
    for load in loads:
        load.start()

    barrier = pltpu.get_barrier_semaphore()
    partners = [sib, *to_x, *to_y, *to_zl[1:], along_z(1), along_z(-1)]
    for partner in partners:
        pl.semaphore_signal(barrier, inc=1, device_id=partner, device_id_type=MESH)
    pl.semaphore_wait(barrier, len(partners))

    def tell(n):
        for partner in (along_z(n), along_z(-n)):
            pl.semaphore_signal(
                known.at[n - 1], inc=1, device_id=partner, device_id_type=MESH
            )

    tell(1)

    sent = []

    def send(src, dst, send_sem, recv_sem, device):
        copy = pltpu.make_async_remote_copy(
            src_ref=src, dst_ref=dst, send_sem=send_sem, recv_sem=recv_sem,
            device_id=device, device_id_type=MESH,
        )
        copy.start()
        sent.append(copy)
        return copy

    az, ax, ac, yy, zz, yg, cc, xx, ff = ({} for _ in range(9))

    def share(k, j, source):
        block = xg.at[k, c, source]
        ac[k, j] = send(block, block, ac_s.at[k, j], ac_r.at[k, j], sib)

    def stage_a(k):
        if k:
            az[k].wait_recv()
        block = xg.at[k, c, x]
        for j in range(3):
            ax[k, j] = send(block, block, ax_s.at[k, j], ax_r.at[k, j], to_x[j])
        if k == 0:
            for i in range(1, K):
                az[i] = send(block, xg.at[i, c, x], az_s.at[i], az_r.at[i], to_zl[i])
        share(k, 3, x)

    def stage_b(k):
        for j, source in enumerate((xs[1], xs[0], xs[2])):
            ax[k, j].wait_recv()
            share(k, j, source)

    def stage_y(k):
        pl.semaphore_wait(known.at[0], 2)
        tell(2)

    def stage_z(k):
        pl.semaphore_wait(known.at[1], 2)

    def stage_c(k):
        for j in range(4):
            ac[k, j].wait_recv()
        if k == 0:
            loads[1].wait()
        rows = xg[k].reshape(128, xg.shape[-1])
        value = jnp.dot(rows, we[...], preferred_element_type=F32)
        pre[k] = value.reshape(pre.shape[1:])
        ps[k] = value.reshape(ps.shape[1:]).astype(BF)
        for j in range(3):
            yy[k, j] = send(ps.at[k, ys[j]], yr.at[k, j], y_s.at[k, j], y_r.at[k, j], to_y[j])

    def stage_d(k):
        for j in range(3):
            yy[k, j].wait_recv()
        value = pre[k, y]
        for j in range(3):
            value = value + yr[k, j].astype(F32)
        s1[k] = value
        zs[k, 0] = value.astype(BF)
        zz[k, 0] = send(zs.at[k, 0], zr.at[k, 0], z_s.at[k, 0], z_r.at[k, 0], to_pair[0])

    def stage_e(k):
        zz[k, 0].wait_recv()
        value = s1[k] + zr[k, 0].astype(F32)
        s1[k] = value
        zs[k, 1] = value.astype(BF)
        zz[k, 1] = send(zs.at[k, 1], zr.at[k, 1], z_s.at[k, 1], z_r.at[k, 1], to_pair[1])

    def stage_f(k):
        zz[k, 1].wait_recv()
        if k == 0:
            loads[3].wait()
        value = s1[k] + zr[k, 1].astype(F32) + be[...]
        cod[k, y] = jnp.maximum(value, 0.0).astype(BF)
        piece = cod.at[k, y]
        for j in range(3):
            yg[k, j] = send(piece, piece, yg_s.at[k, j], yg_r.at[k, j], to_y[j])

    def stage_g(k):
        for j in range(3):
            yg[k, j].wait_recv()
        if k == 0:
            loads[2].wait()
        codes = cod[k].reshape(128, cod.shape[-1])
        part = jnp.dot(codes, wd[...], preferred_element_type=F32)
        pb[k] = part.astype(BF).reshape(pb.shape[1:])
        cc[k] = send(pb.at[k, 1 - c], sr.at[k], c_s.at[k], c_r.at[k], sib)

    def stage_h(k):
        cc[k].wait_recv()
        qb[k] = (pb[k, c].astype(F32) + sr[k].astype(F32)).astype(BF)
        for j in range(3):
            xx[k, j] = send(qb.at[k, xs[j]], xr.at[k, j], x_s.at[k, j], x_r.at[k, j], to_x[j])

    def stage_i(k):
        for j in range(3):
            xx[k, j].wait_recv()
        value = qb[k, x].astype(F32)
        for j in range(3):
            value = value + xr[k, j].astype(F32)
        if k == 0:
            acc[...] = value
        else:
            rb[k] = value.astype(BF)
            ff[k] = send(rb.at[k], fr.at[k], f_s.at[k], f_r.at[k], to_zl[k])

    stages = {
        "A": stage_a, "B": stage_b, "C": stage_c, "D": stage_d, "E": stage_e,
        "F": stage_f, "G": stage_g, "H": stage_h, "I": stage_i,
        "Y": stage_y, "Z": stage_z,
    }
    loads[0].wait()
    for step in ORDER:
        stages[step[0]](int(step[1]))

    loads[4].wait()
    value = acc[...] + bd[...]
    for k in range(1, K):
        ff[k].wait_recv()
        value = value + fr[k].astype(F32)
    out[...] = value.astype(BF)
    for copy in sent:
        copy.wait_send()


def on_device(acts, enc_weight, enc_bias, dec_weight, dec_bias):
    rows, _, width = acts.shape
    panel = enc_weight.shape[2]
    dma = pltpu.SemaphoreType.DMA
    pairs = lambda *shape: [dma(shape), dma(shape)]
    result = pl.pallas_call(
        kernel,
        name="crosscoder",
        out_shape=jax.ShapeDtypeStruct((rows, width), BF),
        in_specs=[pl.BlockSpec(memory_space=pl.ANY)] * 5,
        out_specs=pl.BlockSpec(memory_space=pltpu.VMEM),
        scratch_shapes=[
            pltpu.VMEM((K, 2, 4, rows, width), BF),
            pltpu.VMEM((width, panel), BF),
            pltpu.VMEM((panel, width), BF),
            pltpu.VMEM((1, panel), F32),
            pltpu.VMEM((1, width), F32),
            pltpu.VMEM((K, 4, 32, panel), F32),
            pltpu.VMEM((K, 4, 32, panel), BF),
            pltpu.VMEM((K, 3, 32, panel), BF),
            pltpu.VMEM((K, 32, panel), F32),
            pltpu.VMEM((K, 2, 32, panel), BF),
            pltpu.VMEM((K, 2, 32, panel), BF),
            pltpu.VMEM((K, 4, 32, panel), BF),
            pltpu.VMEM((K, 2, 4, rows, width), BF),
            pltpu.VMEM((K, 4, rows, width), BF),
            pltpu.VMEM((K, 4, rows, width), BF),
            pltpu.VMEM((K, 3, rows, width), BF),
            pltpu.VMEM((K, rows, width), BF),
            pltpu.VMEM((K, rows, width), BF),
            pltpu.VMEM((rows, width), F32),
            dma((5,)),
            pltpu.SemaphoreType.REGULAR((2,)),
            *pairs(K), *pairs(K, 3), *pairs(K, 4), *pairs(K, 3), *pairs(K, 2),
            *pairs(K, 3), *pairs(K), *pairs(K, 3), *pairs(K),
        ],
        compiler_params=pltpu.CompilerParams(collective_id=0, has_side_effects=True),
    )(
        acts.reshape(rows, width),
        enc_weight.reshape(width, panel),
        enc_bias.reshape(1, panel),
        dec_weight.reshape(panel, width),
        dec_bias.reshape(1, width),
    )
    return result.reshape(rows, 1, width)


def solution(mesh):
    return jax.shard_map(
        on_device,
        mesh=mesh,
        in_specs=(
            P("latent", "layer", None),
            P("layer", None, "latent"),
            P("latent"),
            P("layer", "latent", None),
            P("layer", None),
        ),
        out_specs=P("latent", "layer", None),
        check_vma=False,
    )
```

time: 182 us -> 68 us (0.37)
  blocking collectives: 107 us -> 0 us
  Pallas kernels: 0 us -> 66.3 us
  waiting for transfers between devices: 53.6 us -> 0 us
  starting transfers between devices: 10.8 us -> 0 us
  matrix products: 4.16 us -> 0 us
  other arithmetic: 2.91 us -> 0 us
    all_to_all x6 -> x0, blocking collectives: 107 us -> none  [the longest x4 70.5 us: copy_for_each(): lax.all_to_all(jnp.broadcast_to(x[None], (count, *x.shape)), axis, 0, 0,...]
    pallas_call x0 -> x1, Pallas kernels: none -> 66.3 us  [on_device(): pl.pallas_call(kernel, name='crosscoder', out_shape=jax.ShapeDtypeStruct(...]
    all_to_all x1 -> x0, waiting for transfers between devices: 53.6 us -> none  [sent_and_summed(): pieces = lax.all_to_all(split_up(x, dim, count), axis, 0, 0, tiled=True)]
    all_to_all x1 -> x0, starting transfers between devices: 10.8 us -> none  [sent_and_summed(): pieces = lax.all_to_all(split_up(x, dim, count), axis, 0, 0, tiled=True)]
    dot_general x2 -> x0, matrix products: 4.16 us -> none  [the longest x1 2.78 us: on_device(): jnp.einsum('tk,lkd->tld', codes, dec_weight, preferred_element_type=jnp.f...]
    reduce_sum x3 -> x0, other arithmetic: 2.11 us -> none  [the longest x2 2.09 us: sent_and_summed(): return jnp.sum(pieces.astype(jnp.float32), axis=0)]
  transfers between devices with their start and end apart: 1 -> 0, of which waited for: 1 -> 0; matrix products, arithmetic and copies ran while one was open for 0% -> 0% of each run, Pallas kernels for 0% -> 0%
where the time goes in v1:
time: 68 us; the launch traced here: 67.9 us
  Pallas kernels  66.3 us (98%)
  local copies, waits for them, and re-layouts  1.52 us (2%)
    pallas_call x1, Pallas kernels, on_device(): pl.pallas_call(kernel, name='crosscoder', out_shape=jax.ShapeDtypeStruct(...  66.3 us
    unnamed x1, local copies, waits for them, and re-layouts  1.52 us

profile of v1, /device:TPU:1, one launch (start us, length us, event | category | flops | bytes accessed | tf_op | source)
XLA Modules:
  0.0 67.9 jit_solution(6059862639154784976)
XLA Ops:
  0.0 66.3 %crosscoder.1 = bf16[16,2304]{1,0:T(8,128)(2,1)} custom-call(bf16[16,2304]{1,0:T(8,128)(2,1)} %bitcast.8, bf16[2304,512]{1,0:T(8,128)(2,1)} %bitcast.5, f32[1,512]{1,0:T(1,128)} %bitcast.9, bf16[512,2304]{1,0:T(8,128)(2,1)} %bitcast.6, f32[1,2304]{1,0:T(1,128)} %bdec.1), custom_call_target="tpu_custom_call" | custom-call | tf_op jit(solution)/shard_map/crosscoder/pallas_call | solution.py:202
  66.3 1.5 %copy.7 = bf16[16,1,2304]{2,0,1:T(8,128)(2,1)} copy(bf16[16,1,2304]{2,0,1:T(8,128)(2,1)} %bitcast.7) | data formatting | bytes 147456

commit v2 on v1

--- a/solution.py
+++ b/solution.py
@@ -9,19 +9,19 @@
 BF, F32 = jnp.bfloat16, jnp.float32
 K = 4
 ORDER = (
-    "A0", "A1", "Y0", "A2", "B0", "C0", "A3", "B1", "C1", "Z0", "D0", "B2", "C2", "D1", "B3", "C3", "E0",
-    "D2", "E1", "D3", "F0", "E2", "F1", "E3", "G0", "F2", "H0", "G1", "F3", "H1", "G2", "I0", "H2", "G3",
-    "I1", "H3", "I2", "I3",
+    "A0", "A1", "Y0", "A2", "C0", "A3", "C1", "Z0", "D0", "C2", "D1", "C3", "E0", "D2", "E1", "D3", "F0",
+    "E2", "F1", "E3", "G0", "F2", "G1", "F3", "I0", "G2", "I1", "G3", "I2", "I3",
 )
 
 
 def kernel(
     acts, wenc, benc, wdec, bdec, out,
-    xg, we, wd, be, bd, pre, ps, yr, s1, zs, zr, cod, pb, sr, qb, xr, rb, fr, acc,
-    local, known, az_s, az_r, ax_s, ax_r, ac_s, ac_r, y_s, y_r, z_s, z_r, yg_s, yg_r,
-    c_s, c_r, x_s, x_r, f_s, f_r,
+    xg, we, wd, be, bd, pre, ps, yr, s1, zs, zr, cod, qb, xr, rb, fr, acc,
+    local, known, w_s, w_r, az_s, az_r, ax_s, ax_r, y_s, y_r, z_s, z_r, yg_s, yg_r,
+    x_s, x_r, f_s, f_r,
 ):
     layer, latent = lax.axis_index("layer"), lax.axis_index("latent")
+    half = we.shape[-1]
     zh, y = lax.div(layer, 4), lax.rem(layer, 4)
     zl, x, c = lax.div(latent, 8), lax.rem(lax.div(latent, 2), 4), lax.rem(latent, 2)
 
@@ -48,7 +48,7 @@
     loads = [
         pltpu.make_async_copy(src, dst, local.at[i])
         for i, (src, dst) in enumerate(
-            ((acts, xg.at[0, c, x]), (wenc, we), (wdec, wd), (benc, be), (bdec, bd))
+            ((acts, xg.at[0, x]), (wenc, we.at[c]), (wdec, wd.at[c]), (benc, be.at[c]), (bdec, bd))
         )
     ]
     for load in loads:
@@ -68,7 +68,7 @@
 
     tell(1)
 
-    sent = []
+    sent, loaded = [], set()
 
     def send(src, dst, send_sem, recv_sem, device):
         copy = pltpu.make_async_remote_copy(
@@ -79,27 +79,26 @@
         sent.append(copy)
         return copy
 
-    az, ax, ac, yy, zz, yg, cc, xx, ff = ({} for _ in range(9))
-
-    def share(k, j, source):
-        block = xg.at[k, c, source]
-        ac[k, j] = send(block, block, ac_s.at[k, j], ac_r.at[k, j], sib)
+    ww, az, ax, yy, zz, yg, xx, ff = ({} for _ in range(8))
+
+    def once(i):
+        if i not in loaded:
+            loaded.add(i)
+            loads[i].wait()
+            if i in ww:
+                ww[i].wait_recv()
 
     def stage_a(k):
         if k:
             az[k].wait_recv()
-        block = xg.at[k, c, x]
+        block = xg.at[k, x]
         for j in range(3):
             ax[k, j] = send(block, block, ax_s.at[k, j], ax_r.at[k, j], to_x[j])
         if k == 0:
             for i in range(1, K):
-                az[i] = send(block, xg.at[i, c, x], az_s.at[i], az_r.at[i], to_zl[i])
-        share(k, 3, x)
-
-    def stage_b(k):
-        for j, source in enumerate((xs[1], xs[0], xs[2])):
-            ax[k, j].wait_recv()
-            share(k, j, source)
+                az[i] = send(block, xg.at[i, x], az_s.at[i], az_r.at[i], to_zl[i])
+            for i, src, dst in ((1, wenc, we), (3, benc, be), (2, wdec, wd)):
+                ww[i] = send(src, dst.at[c], w_s.at[i], w_r.at[i], sib)
 
     def stage_y(k):
         pl.semaphore_wait(known.at[0], 2)
@@ -109,14 +108,15 @@
         pl.semaphore_wait(known.at[1], 2)
 
     def stage_c(k):
-        for j in range(4):
-            ac[k, j].wait_recv()
-        if k == 0:
-            loads[1].wait()
-        rows = xg[k].reshape(128, xg.shape[-1])
-        value = jnp.dot(rows, we[...], preferred_element_type=F32)
-        pre[k] = value.reshape(pre.shape[1:])
-        ps[k] = value.reshape(ps.shape[1:]).astype(BF)
+        for j in range(3):
+            ax[k, j].wait_recv()
+        once(1)
+        lines = xg[k].reshape(-1, xg.shape[-1])
+        for i in range(2):
+            value = jnp.dot(lines, we[i], preferred_element_type=F32)
+            value = value.reshape(4, -1, half)
+            pre[k, :, :, i * half : (i + 1) * half] = value
+            ps[k, :, :, i * half : (i + 1) * half] = value.astype(BF)
         for j in range(3):
             yy[k, j] = send(ps.at[k, ys[j]], yr.at[k, j], y_s.at[k, j], y_r.at[k, j], to_y[j])
 
@@ -139,9 +139,9 @@
 
     def stage_f(k):
         zz[k, 1].wait_recv()
-        if k == 0:
-            loads[3].wait()
-        value = s1[k] + zr[k, 1].astype(F32) + be[...]
+        once(3)
+        bias = jnp.concatenate([be[0], be[1]], axis=1)
+        value = s1[k] + zr[k, 1].astype(F32) + bias
         cod[k, y] = jnp.maximum(value, 0.0).astype(BF)
         piece = cod.at[k, y]
         for j in range(3):
@@ -150,17 +150,12 @@
     def stage_g(k):
         for j in range(3):
             yg[k, j].wait_recv()
-        if k == 0:
-            loads[2].wait()
-        codes = cod[k].reshape(128, cod.shape[-1])
-        part = jnp.dot(codes, wd[...], preferred_element_type=F32)
-        pb[k] = part.astype(BF).reshape(pb.shape[1:])
-        cc[k] = send(pb.at[k, 1 - c], sr.at[k], c_s.at[k], c_r.at[k], sib)
-
-    def stage_h(k):
-        cc[k].wait_recv()
-        qb[k] = (pb[k, c].astype(F32) + sr[k].astype(F32)).astype(BF)
-        for j in range(3):
+        once(2)
+        codes = cod[k].reshape(-1, 2 * half)
+        part = jnp.dot(codes[:, :half], wd[0], preferred_element_type=F32)
+        part = part + jnp.dot(codes[:, half:], wd[1], preferred_element_type=F32)
+        qb[k] = part.astype(BF).reshape(qb.shape[1:])
+        for j in (2, 0, 1):
             xx[k, j] = send(qb.at[k, xs[j]], xr.at[k, j], x_s.at[k, j], x_r.at[k, j], to_x[j])
 
     def stage_i(k):
@@ -176,15 +171,14 @@
             ff[k] = send(rb.at[k], fr.at[k], f_s.at[k], f_r.at[k], to_zl[k])
 
     stages = {
-        "A": stage_a, "B": stage_b, "C": stage_c, "D": stage_d, "E": stage_e,
-        "F": stage_f, "G": stage_g, "H": stage_h, "I": stage_i,
-        "Y": stage_y, "Z": stage_z,
+        "A": stage_a, "C": stage_c, "D": stage_d, "E": stage_e,
+        "F": stage_f, "G": stage_g, "I": stage_i, "Y": stage_y, "Z": stage_z,
     }
-    loads[0].wait()
+    once(0)
     for step in ORDER:
         stages[step[0]](int(step[1]))
 
-    loads[4].wait()
+    once(4)
     value = acc[...] + bd[...]
     for k in range(1, K):
         ff[k].wait_recv()
@@ -206,20 +200,18 @@
         in_specs=[pl.BlockSpec(memory_space=pl.ANY)] * 5,
         out_specs=pl.BlockSpec(memory_space=pltpu.VMEM),
         scratch_shapes=[
-            pltpu.VMEM((K, 2, 4, rows, width), BF),
-            pltpu.VMEM((width, panel), BF),
-            pltpu.VMEM((panel, width), BF),
-            pltpu.VMEM((1, panel), F32),
+            pltpu.VMEM((K, 4, rows, width), BF),
+            pltpu.VMEM((2, width, panel), BF),
+            pltpu.VMEM((2, panel, width), BF),
+            pltpu.VMEM((2, 1, panel), F32),
             pltpu.VMEM((1, width), F32),
-            pltpu.VMEM((K, 4, 32, panel), F32),
-            pltpu.VMEM((K, 4, 32, panel), BF),
-            pltpu.VMEM((K, 3, 32, panel), BF),
-            pltpu.VMEM((K, 32, panel), F32),
-            pltpu.VMEM((K, 2, 32, panel), BF),
-            pltpu.VMEM((K, 2, 32, panel), BF),
-            pltpu.VMEM((K, 4, 32, panel), BF),
-            pltpu.VMEM((K, 2, 4, rows, width), BF),
-            pltpu.VMEM((K, 4, rows, width), BF),
+            pltpu.VMEM((K, 4, rows, 2 * panel), F32),
+            pltpu.VMEM((K, 4, rows, 2 * panel), BF),
+            pltpu.VMEM((K, 3, rows, 2 * panel), BF),
+            pltpu.VMEM((K, rows, 2 * panel), F32),
+            pltpu.VMEM((K, 2, rows, 2 * panel), BF),
+            pltpu.VMEM((K, 2, rows, 2 * panel), BF),
+            pltpu.VMEM((K, 4, rows, 2 * panel), BF),
             pltpu.VMEM((K, 4, rows, width), BF),
             pltpu.VMEM((K, 3, rows, width), BF),
             pltpu.VMEM((K, rows, width), BF),
@@ -227,8 +219,8 @@
             pltpu.VMEM((rows, width), F32),
             dma((5,)),
             pltpu.SemaphoreType.REGULAR((2,)),
-            *pairs(K), *pairs(K, 3), *pairs(K, 4), *pairs(K, 3), *pairs(K, 2),
-            *pairs(K, 3), *pairs(K), *pairs(K, 3), *pairs(K),
+            *pairs(K), *pairs(K), *pairs(K, 3), *pairs(K, 3), *pairs(K, 2),
+            *pairs(K, 3), *pairs(K, 3), *pairs(K),
         ],
         compiler_params=pltpu.CompilerParams(collective_id=0, has_side_effects=True),
     )(

time: 68 us -> 64.6 us (0.950)
  the two profiles are of different devices: /device:TPU:1 before, /device:TPU:2 now
where the time goes in v2:
time: 64.6 us; the launch traced here: 64.5 us
  Pallas kernels  63 us (98%)
  local copies, waits for them, and re-layouts  1.52 us (2%)
    pallas_call x1, Pallas kernels, on_device(): pl.pallas_call(kernel, name='crosscoder', out_shape=jax.ShapeDtypeStruct(...  63 us
    unnamed x1, local copies, waits for them, and re-layouts  1.52 us

profile of v2, /device:TPU:2, one launch (start us, length us, event | category | flops | bytes accessed | tf_op | source)
XLA Modules:
  0.0 64.5 jit_solution(227335572649139346)
XLA Ops:
  0.0 63.0 %crosscoder.1 = bf16[16,2304]{1,0:T(8,128)(2,1)} custom-call(bf16[16,2304]{1,0:T(8,128)(2,1)} %bitcast.8, bf16[2304,512]{1,0:T(8,128)(2,1)} %bitcast.5, f32[1,512]{1,0:T(1,128)} %bitcast.9, bf16[512,2304]{1,0:T(8,128)(2,1)} %bitcast.6, f32[1,2304]{1,0:T(1,128)} %bdec.1), custom_call_target="tpu_custom_call" | custom-call | tf_op jit(solution)/shard_map/crosscoder/pallas_call | solution.py:196
  63.0 1.5 %copy.7 = bf16[16,1,2304]{2,0,1:T(8,128)(2,1)} copy(bf16[16,1,2304]{2,0,1:T(8,128)(2,1)} %bitcast.7) | data formatting | bytes 147456

commit v3 on v2

--- a/solution.py
+++ b/solution.py
@@ -92,7 +92,7 @@
         if k:
             az[k].wait_recv()
         block = xg.at[k, x]
-        for j in range(3):
+        for j in (2, 0, 1):
             ax[k, j] = send(block, block, ax_s.at[k, j], ax_r.at[k, j], to_x[j])
         if k == 0:
             for i in range(1, K):
@@ -117,7 +117,7 @@
             value = value.reshape(4, -1, half)
             pre[k, :, :, i * half : (i + 1) * half] = value
             ps[k, :, :, i * half : (i + 1) * half] = value.astype(BF)
-        for j in range(3):
+        for j in (2, 0, 1):
             yy[k, j] = send(ps.at[k, ys[j]], yr.at[k, j], y_s.at[k, j], y_r.at[k, j], to_y[j])
 
     def stage_d(k):
@@ -144,7 +144,7 @@
         value = s1[k] + zr[k, 1].astype(F32) + bias
         cod[k, y] = jnp.maximum(value, 0.0).astype(BF)
         piece = cod.at[k, y]
-        for j in range(3):
+        for j in (2, 0, 1):
             yg[k, j] = send(piece, piece, yg_s.at[k, j], yg_r.at[k, j], to_y[j])
 
     def stage_g(k):
@@ -193,6 +193,7 @@
     panel = enc_weight.shape[2]
     dma = pltpu.SemaphoreType.DMA
     pairs = lambda *shape: [dma(shape), dma(shape)]
+    held = lambda v: pltpu.with_memory_space_constraint(v, pltpu.HBM)
     result = pl.pallas_call(
         kernel,
         name="crosscoder",
@@ -222,13 +223,13 @@
             *pairs(K), *pairs(K), *pairs(K, 3), *pairs(K, 3), *pairs(K, 2),
             *pairs(K, 3), *pairs(K, 3), *pairs(K),
         ],
-        compiler_params=pltpu.CompilerParams(collective_id=0, has_side_effects=True),
+        compiler_params=pltpu.CompilerParams(collective_id=0, has_side_effects=True, vmem_limit_bytes=48*1024*1024),
     )(
-        acts.reshape(rows, width),
-        enc_weight.reshape(width, panel),
-        enc_bias.reshape(1, panel),
-        dec_weight.reshape(panel, width),
-        dec_bias.reshape(1, width),
+        held(acts.reshape(rows, width)),
+        held(enc_weight.reshape(width, panel)),
+        held(enc_bias.reshape(1, panel)),
+        held(dec_weight.reshape(panel, width)),
+        held(dec_bias.reshape(1, width)),
     )
     return result.reshape(rows, 1, width)
 

time: 64.6 us -> 62.7 us (0.971)
  Pallas kernels: 63 us -> 61.9 us
  local copies, waits for them, and re-layouts: 1.52 us -> 0.64 us
    pallas_call x1, Pallas kernels: 63 us -> 61.9 us  [on_device(): pl.pallas_call(kernel, name='crosscoder', out_shape=jax.ShapeDtypeStruct(...]
    unnamed x1, local copies, waits for them, and re-layouts: 1.52 us -> 0.64 us
where the time goes in v3:
time: 62.7 us; the launch traced here: 62.6 us
  Pallas kernels  61.9 us (99%)
  local copies, waits for them, and re-layouts  0.64 us (1%)
    pallas_call x1, Pallas kernels, on_device(): pl.pallas_call(kernel, name='crosscoder', out_shape=jax.ShapeDtypeStruct(...  61.9 us

profile of v3, /device:TPU:2, one launch (start us, length us, event | category | flops | bytes accessed | tf_op | source)
XLA Modules:
  0.0 62.6 jit_solution(12647542665212968290)
XLA Ops:
  0.0 61.9 %crosscoder.1 = bf16[16,2304]{1,0:T(8,128)(2,1)S(1)} custom-call(bf16[16,2304]{1,0:T(8,128)(2,1)} %bitcast.8, bf16[2304,512]{1,0:T(8,128)(2,1)} %bitcast.6, f32[1,512]{1,0:T(1,128)} %bitcast.9, bf16[512,2304]{1,0:T(8,128)(2,1)} %bitcast.7, f32[1,2304]{1,0:T(1,128)} %bdec.1), custom_call_target="tpu_custom_call" | custom-call | tf_op jit(solution)/shard_map/crosscoder/pallas_call | solution.py:197
  61.9 0.6 %copy.7 = bf16[16,1,2304]{2,0,1:T(8,128)(2,1)} copy(bf16[16,1,2304]{2,0,1:T(8,128)(2,1)S(1)} %bitcast.5) | data formatting | bytes 147456
